TPU v7x, 512 devices: a whole 4x8x8 slice. The times are simulated.
512 devices in a mesh: dp: 8 (over y), seq: 64 (over z, x, core).
Axes of the slice: x: 4, y: 8, z: 8, core: 2. Of those that a mesh axis runs over, the one named last changes fastest.
Arguments:
- mel_frames: bfloat16 [8, 16384, 128], P('dp', 'seq'), may hold values from -16 to 16
- positions: int32 [8, 8192], P('dp', 'seq'), may hold values from 0 to 16383, as said below
- conv_weight: bfloat16 [128, 3, 1280], replicated, may hold values from -0.3125 to 0.3125
- conv_bias: float32 [1280], replicated, may hold values from -3 to 3
- proj_weight: bfloat16 [1280, 2048], P('dp'), may hold values from -0.15625 to 0.15625
- proj_bias: float32 [2048], replicated, may hold values from -3 to 3
- cotangent: bfloat16 [8, 16384, 2048], P('dp', 'seq'), may hold values from -0.032958984 to 0.032958984
Outputs:
- merged: bfloat16 [8, 16384, 2048], P('dp', 'seq')
- grad_weight: float32 [128, 3, 1280], P('seq', None, 'dp')
Inputs may be any that keep to these rules, and one draw needn't show every extreme that they name: Within a recording the 8192 entries are distinct. Block b of the sequence is positions b * 256 to b * 256 + 255; the 128 tokens of one window put at most 4 entries into any one block, and in each recording one block receives exactly 4 from every window.
All inputs are finite; a program needn't handle non-finite values.
Results may differ from a plain program's by a relative error of at most 0.012.
Values may be sent and summed in bfloat16 or wider, within the bound.
A program may use at most 64 MiB of HBM per device.

v0:
```python
import jax
import jax.numpy as jnp
from jax import lax
from jax.sharding import PartitionSpec as P

SQRT_HALF = 0.7071067811865476
INV_SQRT_TWO_PI = 0.3989422804014327


def gelu_value(x):
    return x * 0.5 * (1.0 + lax.erf(x * SQRT_HALF))


def gelu_slope(x):
    return 0.5 * (1.0 + lax.erf(x * SQRT_HALF)) + x * INV_SQRT_TWO_PI * jnp.exp(-0.5 * x * x)


def body(mel_frames, positions, conv_weight, conv_bias, proj_weight, proj_bias, cotangent):
    frames = mel_frames[0]
    local_spots = positions[0]
    grads_in = cotangent[0]
    owner_count = lax.axis_size("seq")
    frame_count = frames.shape[0]
    tok_count = frame_count // 2
    rows_own = grads_in.shape[0]
    capacity = rows_own // owner_count
    tap_count = conv_weight.shape[1]
    channels = conv_weight.shape[2]
    padded = jnp.pad(frames, ((1, 1), (0, 0)))
    stacked = jnp.concatenate([padded[k : k + frame_count] for k in range(tap_count)], axis=1)
    kernel = jnp.transpose(conv_weight, (1, 0, 2)).reshape(-1, channels)
    pre_act = jnp.dot(stacked, kernel, preferred_element_type=jnp.float32) + conv_bias
    act_pairs = gelu_value(pre_act).reshape(tok_count, 2, channels)
    pooled = (0.5 * (act_pairs[:, 0, :] + act_pairs[:, 1, :])).astype(jnp.bfloat16)
    full_weight = lax.all_gather(proj_weight, "dp", axis=0, tiled=True)
    owner_index = local_spots // rows_own
    owner_row = local_spots % rows_own
    onehot = (owner_index[:, None] == jnp.arange(owner_count, dtype=jnp.int32)[None, :]).astype(
        jnp.int32
    )
    rank_before = jnp.cumsum(onehot, axis=0) - onehot
    slot_rank = jnp.sum(rank_before * onehot, axis=1)
    slot_index = owner_index * capacity + slot_rank
    dest_rows = (
        jnp.full((owner_count * capacity,), rows_own, jnp.int32).at[slot_index].set(owner_row)
    )
    dest_rows = dest_rows.reshape(owner_count, capacity)
    contract_last = (((1,), (1,)), ((), ()))
    projected = (
        jnp.dot(pooled, full_weight, preferred_element_type=jnp.float32) + proj_bias
    ).astype(jnp.bfloat16)
    outgoing = (
        jnp.zeros((owner_count * capacity, projected.shape[1]), jnp.bfloat16)
        .at[slot_index]
        .set(projected)
    )
    outgoing = outgoing.reshape(owner_count, capacity, -1)
    arrived, arrived_rows = (
        lax.all_to_all(outgoing, "seq", split_axis=0, concat_axis=0, tiled=True),
        lax.all_to_all(dest_rows, "seq", split_axis=0, concat_axis=0, tiled=True),
    )
    flat_rows = arrived_rows.reshape(-1)
    merged = (
        jnp.zeros_like(grads_in)
        .at[flat_rows]
        .set(arrived.reshape(flat_rows.shape[0], -1), mode="drop")
    )
    picked = jnp.take(grads_in, flat_rows, axis=0, mode="clip").reshape(owner_count, capacity, -1)
    returned = lax.all_to_all(picked, "seq", split_axis=0, concat_axis=0, tiled=True)
    grad_tokens = returned.reshape(owner_count * capacity, -1)[slot_index]
    grad_pooled = lax.dot_general(
        grad_tokens, full_weight, contract_last, preferred_element_type=jnp.float32
    ).astype(jnp.bfloat16)
    slopes = gelu_slope(pre_act).reshape(tok_count, 2, channels)
    grad_pre = (0.5 * grad_pooled.astype(jnp.float32)[:, None, :] * slopes).astype(jnp.bfloat16)
    grad_pre = grad_pre.reshape(frame_count, channels)
    contract_first = (((0,), (0,)), ((), ()))
    tap_terms = [
        lax.dot_general(
            padded[k : k + frame_count],
            grad_pre,
            contract_first,
            preferred_element_type=jnp.float32,
        )
        for k in range(tap_count)
    ]
    seq_share = lax.psum_scatter(
        jnp.stack(tap_terms, axis=1), "seq", scatter_dimension=0, tiled=True
    )
    grad_weight = lax.psum_scatter(seq_share, "dp", scatter_dimension=2, tiled=True)
    return (merged[None], grad_weight)


def solution(mesh):
    in_specs = (
        P("dp", "seq", None),
        P("dp", "seq"),
        P(),
        P(),
        P("dp", None),
        P(),
        P("dp", "seq", None),
    )
    out_specs = (P("dp", "seq", None), P("seq", None, "dp"))
    return jax.shard_map(body, mesh=mesh, in_specs=in_specs, out_specs=out_specs, check_vma=False)
```

profile of v0, /device:TPU:2, one launch (start us, length us, event | category | flops | bytes accessed | tf_op | source)
XLA Modules:
  0.0 377.3 jit_solution(8471840743982743471)
XLA Ops:
  7.2 0.0 all-gather.2.cloned.1.call-start
  7.2 0.7 all-gather.2.cloned.1.call-update
  7.9 0.7 and_select_fusion
  8.6 0.1 fusion.22
  8.7 0.2 reduce_window_sum.11
  8.8 0.2 select_reduce_fusion
  9.0 0.7 fusion.23
  9.7 1.0 scatter_custom_fusion
  10.7 0.1 all_to_all.12
  10.8 22.3 %all_to_all.19 = s32[64,1,4]{2,1,0:T(1,128)S(1)} all-to-all(s32[64,1,4]{2,1,0:T(1,128)S(1)} %bitcast.73), channel_id=1, replica_groups=mesh['dp'=8,'seq'=64] {'seq'}, dimensions={0} | all-to-all | bytes 2048 | tf_op jit(solution)/shard_map/all_to_all | solution.py:60
  33.1 0.1 reshape.178
  33.2 1.4 gather_fusion
  34.5 1.2 reshape.174
  35.8 5.7 %all-to-all-start.2 = ((bf16[64,4,2048]{2,1,0:T(4,128)(2,1)}), bf16[64,4,2048]{2,1,0:T(4,128)(2,1)S(1)}, u32[]{:S(2)}, u32[]{:S(2)}) async-start(bf16[64,4,2048]{2,1,0:T(4,128)(2,1)} %reshape.174), calls=%async_computation.2 | async-start | bytes 2097152 | tf_op jit(solution)/shard_map/all_to_all | solution.py:69
  41.5 28.8 %all-to-all-done.2 = bf16[64,4,2048]{2,1,0:T(4,128)(2,1)S(1)} async-done(((bf16[64,4,2048]{2,1,0:T(4,128)(2,1)}), bf16[64,4,2048]{2,1,0:T(4,128)(2,1)S(1)}, u32[]{:S(2)}, u32[]{:S(2)}) %all-to-all-start.2) | async-done | bytes 1048608 | tf_op jit(solution)/shard_map/all_to_all | solution.py:69
  70.4 0.3 reshape.175
  70.6 0.9 gather_fusion.1
  71.6 10.2 %all-gather.2.cloned.1.call-done = bf16[1280,2048]{1,0:T(8,128)(2,1)} async-done(((bf16[160,2048]{1,0:T(8,128)(2,1)}), bf16[1280,2048]{1,0:T(8,128)(2,1)}) %all-gather.2.cloned.1.call-update) | async-done | bytes 5242896 | tf_op jit(solution)/shard_map/all_gather | solution.py:35
  81.7 4.3 %fusion.2 = f32[128,1280]{1,0:T(8,128)S(1)} fusion(bf16[128,2048]{1,0:T(8,128)(2,1)S(1)} %gather_fusion.1, bf16[1280,2048]{1,0:T(8,128)(2,1)} %all-gather.2.cloned.1.call-done), kind=kOutput, calls=%fused_computation.13 | convolution fusion | flops 671580160 | bytes 6422528 | tf_op jit(solution)/shard_map/dot_general | solution.py:71
  86.1 0.5 mul.82
  86.5 2.0 mul.83
  88.6 3.6 fusion.7
  92.1 2.1 reshape.171
  94.2 1.0 fusion.29
  95.2 4.2 %fusion = bf16[128,2048]{1,0:T(8,128)(2,1)} fusion(bf16[1280,2048]{1,0:T(8,128)(2,1)} %all-gather.2.cloned.1.call-done, f32[2048]{0:T(1024)S(1)} %copy-done.2, f32[128,1,1280]{2,1,0:T(1,128)S(1)} %get-tuple-element.5, f32[128,1,1280]{2,1,0:T(1,128)S(1)} %get-tuple-element.4), kind=kOutput, calls=%fused_computation.10 | convolution fusion | flops 672104448 | bytes 7086080 | tf_op jit(solution)/shard_map/dot_general | solution.py:50
  99.4 2.4 scatter_custom_fusion.1
  101.8 1.2 reshape.172
  103.1 10.9 %all-to-all-start.1 = ((bf16[64,4,2048]{2,1,0:T(4,128)(2,1)}), bf16[64,4,2048]{2,1,0:T(4,128)(2,1)S(1)}, u32[]{:S(2)}, u32[]{:S(2)}) async-start(bf16[64,4,2048]{2,1,0:T(4,128)(2,1)} %reshape.172), calls=%async_computation.1 | async-start | bytes 2097152 | tf_op jit(solution)/shard_map/all_to_all | solution.py:59
  114.0 0.0 all-reduce.4.cloned.1.call-start
  114.0 0.3 convolution_bitcast_fusion
  114.3 0.3 convolution_bitcast_fusion.2
  114.6 0.3 convolution_bitcast_fusion.1
  114.9 1.4 pad_maximum_fusion
  116.3 0.0 reduce-scatter.5.cloned.1.call-start
  116.4 1.3 dynamic-slice
  118.3 0.5 broadcast.196
  118.8 0.7 reduce.5
  119.6 0.1 reshape.169
  119.7 199.2 %all-reduce.4.cloned.1.call-done = f32[128,3,1280]{2,0,1:T(8,128)} async-done(((f32[128,3,1280]{2,0,1:T(8,128)}), f32[128,3,1280]{2,0,1:T(8,128)}) %all-reduce.4.cloned.1.call-update) | async-done | bytes 1966096
  318.8 0.9 constant_dynamic-slice_fusion
  319.8 2.0 copy.20
  321.8 3.8 reshape.219
  325.5 0.0 reduce-scatter.5.cloned.1.call-update
  325.5 38.5 %reduce-scatter.5.cloned.1.call-done = f32[160,6]{1,0:T(8,128)} async-done(((f32[1280,6]{1,0:T(8,128)}), f32[160,6]{1,0:T(8,128)}) %reduce-scatter.5.cloned.1.call-update) | async-done | bytes 3856
  364.0 1.1 reshape.220
  365.1 0.8 copy.21
  365.8 1.1 reshape.212
  366.9 3.8 %scatter_custom_fusion.2 = bf16[256,2048]{1,0:T(8,128)(2,1)} fusion(s32[256]{0:T(256)S(1)} %bitcast.74, bf16[256,2048]{1,0:T(8,128)(2,1)} %reshape.212, bf16[]{:T(256)} %constant.25.clone.1), kind=kCustom, calls=%fused_computation.26 | custom fusion | bytes 1049088 | tf_op jit(solution)/shard_map/scatter | solution.py:66
  (14 shorter events, 0.1 us)
Async XLA Ops:
  7.2 26.0 %copy-start = (bf16[1,256,2048]{2,1,0:T(8,128)(2,1)S(1)}, bf16[1,256,2048]{2,1,0:T(8,128)(2,1)}, u32[]{:S(2)}) copy-start(bf16[1,256,2048]{2,1,0:T(8,128)(2,1)} %param.13) | copy-start | bytes 3145732
  7.2 74.5 %all-gather.2.cloned.1.call-start = ((), (), s32[]{:S(2)}) async-start(), calls=%async_computation.4 | async-start | bytes 5898240 | tf_op jit(solution)/shard_map/all_gather | solution.py:35
  35.8 5.7 %copy-start.1 = (bf16[1,256,128]{2,1,0:T(8,128)(2,1)S(1)}, bf16[1,256,128]{2,1,0:T(8,128)(2,1)}, u32[]{:S(2)}) copy-start(bf16[1,256,128]{2,1,0:T(8,128)(2,1)} %param.7) | copy-start | bytes 196612
  35.8 34.6 %all-to-all-start.2 = ((bf16[64,4,2048]{2,1,0:T(4,128)(2,1)}), bf16[64,4,2048]{2,1,0:T(4,128)(2,1)S(1)}, u32[]{:S(2)}, u32[]{:S(2)}) async-start(bf16[64,4,2048]{2,1,0:T(4,128)(2,1)} %reshape.174), calls=%async_computation.2 | async-start | bytes 2097152 | tf_op jit(solution)/shard_map/all_to_all | solution.py:69
  86.5 2.0 copy-start.3
  94.2 1.0 copy-start.2
  103.1 262.8 %all-to-all-start.1 = ((bf16[64,4,2048]{2,1,0:T(4,128)(2,1)}), bf16[64,4,2048]{2,1,0:T(4,128)(2,1)S(1)}, u32[]{:S(2)}, u32[]{:S(2)}) async-start(bf16[64,4,2048]{2,1,0:T(4,128)(2,1)} %reshape.172), calls=%async_computation.1 | async-start | bytes 2097152 | tf_op jit(solution)/shard_map/all_to_all | solution.py:59
  114.0 204.9 %all-reduce.4.cloned.1.call-start = ((), (), s32[]{:S(2)}) async-start(), calls=%async_computation.6 | async-start | bytes 3932160
  116.3 247.7 %reduce-scatter.5.cloned.1.call-start = ((), (), s32[]{:S(2)}) async-start(), calls=%async_computation.5 | async-start | bytes 737280
Sparse Core Ops, SparseCore 0:
  10.1 71.5 all-gather.1
  118.2 200.5 all-reduce.3
  325.7 38.3 reduce-scatter.4
where the time goes:
time: 378 us; the launch traced here: 377 us
  waiting for transfers between devices  277 us (73%)
  local copies, waits for them, and re-layouts  29.4 us (8%)
  blocking collectives  22.3 us (6%)
  starting transfers between devices  16.7 us (4%)
  between operations  14.6 us (4%)
  matrix products  12.9 us (3%)
  other arithmetic  3.93 us (1%)
    unnamed x5, waiting for transfers between devices  238 us
    all_to_all x1, waiting for transfers between devices, body(): lax.all_to_all(picked, 'seq', split_axis=0, concat_axis=0, tiled=True)  28.8 us
    all_to_all x1, blocking collectives, body(): lax.all_to_all(dest_rows, 'seq', split_axis=0, concat_axis=0, tiled=True)  22.3 us
    all_to_all x1, starting transfers between devices, body(): lax.all_to_all(outgoing, 'seq', split_axis=0, concat_axis=0, tiled=True)  10.9 us
    all_gather x1, waiting for transfers between devices, body(): full_weight = lax.all_gather(proj_weight, 'dp', axis=0, tiled=True)  10.2 us
    unnamed x14, local copies, waits for them, and re-layouts  9.77 us
  transfers between devices with their start and end apart: 5, of which 4 were waited for; matrix products, arithmetic and copies ran while one was open for 5% of the time, Pallas kernels for 0%

commit v1 on v0

--- a/solution.py
+++ b/solution.py
@@ -32,7 +32,9 @@
     pre_act = jnp.dot(stacked, kernel, preferred_element_type=jnp.float32) + conv_bias
     act_pairs = gelu_value(pre_act).reshape(tok_count, 2, channels)
     pooled = (0.5 * (act_pairs[:, 0, :] + act_pairs[:, 1, :])).astype(jnp.bfloat16)
-    full_weight = lax.all_gather(proj_weight, "dp", axis=0, tiled=True)
+    full_weight = jnp.concatenate(
+        lax.all_to_all(jnp.stack([proj_weight] * lax.axis_size("dp")), "dp", 0, 0), axis=0
+    )
     owner_index = local_spots // rows_own
     owner_row = local_spots % rows_own
     onehot = (owner_index[:, None] == jnp.arange(owner_count, dtype=jnp.int32)[None, :]).astype(

time: 378 us -> 487 us (1.29)
  waiting for transfers between devices: 277 us -> 352 us
  blocking collectives: 22.3 us -> 56.9 us
    all_to_all x1, waiting for transfers between devices: 28.8 us -> 117 us  [body(): lax.all_to_all(jnp.stack([proj_weight] * lax.axis_size('dp')), 'dp', 0, 0)]
    all_to_all x0 -> x1, blocking collectives: none -> 34.6 us  [body(): lax.all_to_all(picked, 'seq', split_axis=0, concat_axis=0, tiled=True)]
    all_gather x1 -> x0, waiting for transfers between devices: 10.2 us -> none  [body(): full_weight = lax.all_gather(proj_weight, 'dp', axis=0, tiled=True)]
    unnamed x5 -> x4, waiting for transfers between devices: 238 us -> 235 us
    unnamed x14 -> x16, local copies, waits for them, and re-layouts: 9.77 us -> 9.77 us
  transfers between devices with their start and end apart: 5 -> 4, of which waited for: 4 -> 3; matrix products, arithmetic and copies ran while one was open for 5% -> 3% of each run, Pallas kernels for 0% -> 0%
where the time goes in v1:
time: 487 us
  waiting for transfers between devices  352 us (72%)
  blocking collectives  56.9 us (12%)
  local copies, waits for them, and re-layouts  32.3 us (7%)
  between operations  14.9 us (3%)
  starting transfers between devices  13.9 us (3%)
  matrix products  12.9 us (3%)
    unnamed x4, waiting for transfers between devices  235 us
    all_to_all x1, waiting for transfers between devices, body(): lax.all_to_all(jnp.stack([proj_weight] * lax.axis_size('dp')), 'dp', 0, 0)  117 us
    all_to_all x1, blocking collectives, body(): lax.all_to_all(picked, 'seq', split_axis=0, concat_axis=0, tiled=True)  34.6 us
    all_to_all x1, blocking collectives, body(): lax.all_to_all(dest_rows, 'seq', split_axis=0, concat_axis=0, tiled=True)  22.3 us
    unnamed x16, local copies, waits for them, and re-layouts  9.77 us
  transfers between devices with their start and end apart: 4, of which 3 were waited for; matrix products, arithmetic and copies ran while one was open for 3% of the time, Pallas kernels for 0%

profile of v1, /device:TPU:2, one launch (start us, length us, event | category | flops | bytes accessed | tf_op | source)
XLA Modules:
  0.0 486.5 jit_solution(15610738796494832421)
XLA Ops:
  7.2 0.8 and_select_fusion
  7.9 0.1 fusion.22
  8.0 0.2 reduce_window_sum.11
  8.2 0.2 select_reduce_fusion
  8.4 0.7 fusion.23
  9.0 1.0 scatter_custom_fusion
  10.0 0.1 all_to_all.15
  10.1 22.3 %all_to_all.24 = s32[64,1,4]{2,1,0:T(1,128)S(1)} all-to-all(s32[64,1,4]{2,1,0:T(1,128)S(1)} %bitcast.74), channel_id=1, replica_groups=mesh['dp'=8,'seq'=64] {'seq'}, dimensions={0} | all-to-all | bytes 2048 | tf_op jit(solution)/shard_map/all_to_all | solution.py:62
  32.4 0.1 reshape.181
  32.5 1.4 gather_fusion
  33.9 1.2 reshape.177
  35.1 34.6 %all_to_all.25 = bf16[64,4,2048]{2,1,0:T(4,128)(2,1)S(1)} all-to-all(bf16[64,4,2048]{2,1,0:T(4,128)(2,1)} %reshape.177), channel_id=1, replica_groups=mesh['dp'=8,'seq'=64] {'seq'}, dimensions={0} | all-to-all | bytes 2097152 | tf_op jit(solution)/shard_map/all_to_all | solution.py:71
  69.8 3.0 stack.10
  72.8 7.2 %all-to-all-start.1 = ((bf16[8,160,2048]{2,1,0:T(8,128)(2,1)}), bf16[8,160,2048]{2,1,0:T(8,128)(2,1)}, u32[]{:S(2)}, u32[]{:S(2)}) async-start(bf16[8,160,2048]{2,1,0:T(8,128)(2,1)} %stack.10), calls=%async_computation.1 | async-start | bytes 10485760 | tf_op jit(solution)/shard_map/all_to_all | solution.py:36
  80.1 0.3 reshape.178
  80.3 0.9 gather_fusion.1
  81.3 116.6 %all-to-all-done.1 = bf16[8,160,2048]{2,1,0:T(8,128)(2,1)} async-done(((bf16[8,160,2048]{2,1,0:T(8,128)(2,1)}), bf16[8,160,2048]{2,1,0:T(8,128)(2,1)}, u32[]{:S(2)}, u32[]{:S(2)}) %all-to-all-start.1) | async-done | bytes 5242912 | tf_op jit(solution)/shard_map/all_to_all | solution.py:36
  197.9 4.3 fusion.2
  202.3 0.5 mul.82
  202.8 2.0 mul.83
  204.8 3.5 fusion.7
  208.3 2.1 reshape.173
  210.4 1.0 fusion.29
  211.4 4.2 fusion
  215.6 2.2 scatter_custom_fusion.1
  217.8 1.2 reshape.175
  219.0 6.4 %all-to-all-start.2 = ((bf16[64,4,2048]{2,1,0:T(4,128)(2,1)}), bf16[64,4,2048]{2,1,0:T(4,128)(2,1)S(1)}, u32[]{:S(2)}, u32[]{:S(2)}) async-start(bf16[64,4,2048]{2,1,0:T(4,128)(2,1)} %reshape.175), calls=%async_computation.2 | async-start | bytes 2097152 | tf_op jit(solution)/shard_map/all_to_all | solution.py:61
  225.4 0.0 all-reduce.4.cloned.1.call-start
  225.5 0.3 convolution_bitcast_fusion
  225.8 0.3 convolution_bitcast_fusion.2
  226.1 0.3 convolution_bitcast_fusion.1
  226.4 1.4 pad_maximum_fusion
  227.8 0.0 all-reduce.4.cloned.1.call-update
  227.8 0.3 reduce-scatter.5.cloned.1.call-start
  228.1 1.3 dynamic-slice
  230.0 0.5 broadcast.197
  230.5 0.7 reduce.5
  231.3 0.1 reshape.171
  231.4 196.4 %all-reduce.4.cloned.1.call-done = f32[128,3,1280]{2,0,1:T(8,128)} async-done(((f32[128,3,1280]{2,0,1:T(8,128)}), f32[128,3,1280]{2,0,1:T(8,128)}) %all-reduce.4.cloned.1.call-update) | async-done | bytes 1966096
  427.8 0.9 constant_dynamic-slice_fusion
  428.7 2.0 copy.20
  430.7 3.8 reshape.222
  434.4 0.0 reduce-scatter.5.cloned.1.call-update
  434.5 38.5 %reduce-scatter.5.cloned.1.call-done = f32[160,6]{1,0:T(8,128)} async-done(((f32[1280,6]{1,0:T(8,128)}), f32[160,6]{1,0:T(8,128)}) %reduce-scatter.5.cloned.1.call-update) | async-done | bytes 3856
  472.9 1.1 reshape.223
  474.0 0.8 copy.21
  474.7 1.1 reshape.215
  475.9 3.8 scatter_custom_fusion.2
  (15 shorter events, 0.1 us)
Async XLA Ops:
  7.2 25.4 %copy-start = (bf16[1,256,2048]{2,1,0:T(8,128)(2,1)S(1)}, bf16[1,256,2048]{2,1,0:T(8,128)(2,1)}, u32[]{:S(2)}) copy-start(bf16[1,256,2048]{2,1,0:T(8,128)(2,1)} %param.13) | copy-start | bytes 3145732
  35.1 34.6 %copy-start.2 = (bf16[160,2048]{1,0:T(8,128)(2,1)S(1)}, bf16[160,2048]{1,0:T(8,128)(2,1)}, u32[]{:S(2)}) copy-start(bf16[160,2048]{1,0:T(8,128)(2,1)} %param.11) | copy-start | bytes 1966084
  72.8 7.2 %copy-start.1 = (bf16[1,256,128]{2,1,0:T(8,128)(2,1)S(1)}, bf16[1,256,128]{2,1,0:T(8,128)(2,1)}, u32[]{:S(2)}) copy-start(bf16[1,256,128]{2,1,0:T(8,128)(2,1)} %param.7) | copy-start | bytes 196612
  72.8 125.2 %all-to-all-start.1 = ((bf16[8,160,2048]{2,1,0:T(8,128)(2,1)}), bf16[8,160,2048]{2,1,0:T(8,128)(2,1)}, u32[]{:S(2)}, u32[]{:S(2)}) async-start(bf16[8,160,2048]{2,1,0:T(8,128)(2,1)} %stack.10), calls=%async_computation.1 | async-start | bytes 10485760 | tf_op jit(solution)/shard_map/all_to_all | solution.py:36
  202.7 2.0 copy-start.4
  210.4 1.0 copy-start.3
  219.0 255.7 %all-to-all-start.2 = ((bf16[64,4,2048]{2,1,0:T(4,128)(2,1)}), bf16[64,4,2048]{2,1,0:T(4,128)(2,1)S(1)}, u32[]{:S(2)}, u32[]{:S(2)}) async-start(bf16[64,4,2048]{2,1,0:T(4,128)(2,1)} %reshape.175), calls=%async_computation.2 | async-start | bytes 2097152 | tf_op jit(solution)/shard_map/all_to_all | solution.py:61
  225.4 202.3 %all-reduce.4.cloned.1.call-start = ((), (), s32[]{:S(2)}) async-start(), calls=%async_computation.6 | async-start | bytes 3932160
  227.8 245.1 %reduce-scatter.5.cloned.1.call-start = ((), (), s32[]{:S(2)}) async-start(), calls=%async_computation.5 | async-start | bytes 737280
Sparse Core Ops, SparseCore 0:
  229.7 197.9 all-reduce.3
  434.6 38.3 reduce-scatter.4
